TPU v7x, 32 devices: a whole 2x2x4 slice. The times are simulated.
32 devices in a mesh: replica: 8 (over y, x, core), shard: 4 (over z).
Axes of the slice: x: 2, y: 2, z: 4, core: 2. Of those that a mesh axis runs over, the one named last changes fastest.
Arguments:
- tokens: bfloat16 [32768, 1024], P(('replica', 'shard')), may hold values from -6 to 6
- seq_start: int32 [32], P(('replica', 'shard')), may hold values from 0 to 1024, as said below
- out_grad: bfloat16 [32768, 1024], P(('replica', 'shard')), may hold values from -6 to 6
- norm_gain: bfloat16 [1024], P('shard'), may hold values from 0.099609375 to 1.8984375
- w_query: bfloat16 [1024, 512], P('shard'), may hold values from -0.1875 to 0.1875
- w_key: bfloat16 [1024, 512], P('shard'), may hold values from -0.1875 to 0.1875
- w_value: bfloat16 [1024, 1024], P('shard'), may hold values from -0.1875 to 0.1875
- w_outgate: bfloat16 [1024, 1024], P('shard'), may hold values from -0.1875 to 0.1875
- w_lowrank: bfloat16 [1024, 16], P('shard'), may hold values from -0.1875 to 0.1875
- w_rank_up: bfloat16 [16, 512], P('shard'), may hold values from -1.5 to 1.5
- gate_bias: bfloat16 [512], P('shard'), may hold values from 0 to 9
- head_gain: bfloat16 [256], P('shard'), may hold values from 0.099609375 to 1.8984375
- w_output: bfloat16 [1024, 1024], P('shard'), may hold values from -0.1875 to 0.1875
- ffn_gain: bfloat16 [1024], P('shard'), may hold values from 0.099609375 to 1.8984375
- w_gate: bfloat16 [1024, 2816], P('shard'), may hold values from -0.1875 to 0.1875
- w_up: bfloat16 [1024, 2816], P('shard'), may hold values from -0.1875 to 0.1875
- w_down: bfloat16 [2816, 1024], P('shard'), may hold values from -0.109375 to 0.109375
Outputs:
- output: bfloat16 [32768, 1024], P(('replica', 'shard'))
- tokens_grad: bfloat16 [32768, 1024], P(('replica', 'shard'))
- norm_gain_grad: float32 [1024], P('shard')
- w_query_grad: float32 [1024, 512], P('shard')
- w_key_grad: float32 [1024, 512], P('shard')
- w_value_grad: float32 [1024, 1024], P('shard')
- w_outgate_grad: float32 [1024, 1024], P('shard')
- w_lowrank_grad: float32 [1024, 16], P('shard')
- w_rank_up_grad: float32 [16, 512], P('shard')
- gate_bias_grad: float32 [512], P('shard')
- head_gain_grad: float32 [256], P('shard')
- w_output_grad: float32 [1024, 1024], P('shard')
- ffn_gain_grad: float32 [1024], P('shard')
- w_gate_grad: float32 [1024, 2816], P('shard')
- w_up_grad: float32 [1024, 2816], P('shard')
- w_down_grad: float32 [2816, 1024], P('shard')
Inputs may be any that keep to these rules, and one draw needn't show every extreme that they name: `seq_start`: 1024 means that no sequence begins on the device; other values are multiples of 64; the first device holds 0; sequences begin only on devices whose index along replica+shard is a multiple of 4, and some of those devices hold no start, so that a sequence may run through several groups of 4 devices.
All inputs are finite; a program needn't handle non-finite values.
Results may differ from a plain program's by a relative error of at most 0.025.
Values may be sent and summed in bfloat16 or wider, within the bound.
A program may use at most 640 MiB of HBM per device.

v0:
```python
import jax
import jax.numpy as jnp
from jax import lax
from jax.sharding import PartitionSpec as P

HEAD_COUNT = 4
DK = 128
VALUE_WIDTH = 256
BLOCK = 64


epsilon = 1e-05
normalizer = 16.0
precise_mode = lax.Precision.HIGH


def carried_in(value, axis, join, neutral):
    place = lax.axis_index(axis)
    gathered = jax.tree.map(
        lambda a, kind: lax.all_gather(a.astype(kind), axis), value, (jnp.bfloat16, jnp.bfloat16)
    )
    state = jax.tree.map(lambda a, e: jnp.zeros_like(a) + jnp.asarray(e, a.dtype), value, neutral)

    def carried_one(hop, state):
        return join(
            state,
            jax.tree.map(
                lambda a, own: lax.dynamic_index_in_dim(a, hop, 0, False).astype(own.dtype),
                gathered,
                value,
            ),
        )

    return lax.fori_loop(0, place, carried_one, state)


def entering(value, axis, join, neutral):
    count = lax.axis_size(axis)
    place = lax.axis_index(axis)
    ahead = count - 1 - place
    gathered = jax.tree.map(
        lambda a, kind: lax.all_gather(a.astype(kind), axis),
        value,
        jax.tree.map(lambda a: jnp.bfloat16 if a.dtype == jnp.float32 else a.dtype, value),
    )
    state = jax.tree.map(lambda a, e: jnp.zeros_like(a) + jnp.asarray(e, a.dtype), value, neutral)

    def entering_one(hop, state):
        source = count - 1 - hop
        return join(
            state,
            jax.tree.map(
                lambda a, own: lax.dynamic_index_in_dim(a, source, 0, False).astype(own.dtype),
                gathered,
                value,
            ),
        )

    return lax.fori_loop(0, ahead, entering_one, state)


def dense(left, right):
    return jnp.dot(left, right, preferred_element_type=jnp.float32)


def dense_back(grad_rows, weight):
    return lax.dot_general(
        grad_rows, weight, (((1,), (1,)), ((), ())), preferred_element_type=jnp.float32
    )


def dense_left(input_rows, grad_rows):
    return lax.dot_general(
        input_rows, grad_rows, (((0,), (0,)), ((), ())), preferred_element_type=jnp.float32
    )


def rms_norm(values, gain):
    return values * lax.rsqrt(jnp.mean(values * values, axis=-1, keepdims=True) + epsilon) * gain


def output_gate(mixed_rows, outgate, head_gain):
    count_of_rows = mixed_rows.shape[0]
    shaped = rms_norm(
        mixed_rows.reshape(count_of_rows, HEAD_COUNT, VALUE_WIDTH), head_gain
    ).reshape(count_of_rows, HEAD_COUNT * VALUE_WIDTH)
    return shaped * jax.nn.silu(outgate)


def swiglu(gate_pre, up_pre):
    return jax.nn.silu(gate_pre) * up_pre


def block_step(entering_state, inputs):
    query_rows, key_rows, rows_of_value, log_decay, reset = inputs
    entering_state = entering_state * (1.0 - reset)
    cumul = jnp.cumsum(log_decay, axis=0)
    block_stop = cumul[-1]
    query_decayed = query_rows * jnp.exp(cumul)
    key_dec = key_rows * jnp.exp(-cumul)
    key_final_decay = key_rows * jnp.exp(block_stop - cumul)
    inter_block_part = jnp.einsum(
        "gqs,qso->gqo", query_decayed, entering_state, precision=precise_mode
    )
    scores = jnp.einsum("ihk,jhk->hij", query_decayed, key_dec, precision=precise_mode)
    causal = jnp.tril(jnp.ones((BLOCK, BLOCK), jnp.float32))
    intra_part = jnp.einsum("hij,jhv->ihv", scores * causal, rows_of_value, precision=precise_mode)
    leaving_state = jnp.exp(block_stop)[:, :, None] * entering_state + jnp.einsum(
        "are,aro->reo", key_final_decay, rows_of_value, precision=precise_mode
    )
    return (leaving_state, inter_block_part + intra_part)


def mixer(query_rows, key_rows, rows_of_value, log_decay, resets, entering_state):
    count_of_rows = query_rows.shape[0]
    block_count = count_of_rows // BLOCK
    shaped = (
        query_rows.reshape(block_count, BLOCK, HEAD_COUNT, DK),
        key_rows.reshape(block_count, BLOCK, HEAD_COUNT, DK),
        rows_of_value.reshape(block_count, BLOCK, HEAD_COUNT, VALUE_WIDTH),
        log_decay.reshape(block_count, BLOCK, HEAD_COUNT, DK),
        resets,
    )
    leaving_state, mixed = lax.scan(jax.checkpoint(block_step), entering_state, shaped)
    return (mixed.reshape(count_of_rows, HEAD_COUNT * VALUE_WIDTH), leaving_state)


def link(earlier, later):
    return (later[0] * earlier[0], later[0][:, :, None] * earlier[1] + later[1])


def per_device(
    tokens,
    seq_start,
    out_grad,
    norm_gain,
    w_query,
    w_key,
    w_value,
    w_outgate,
    w_lowrank,
    w_rank_up,
    gate_bias,
    head_gain,
    w_output,
    ffn_gain,
    w_gate,
    w_up,
    w_down,
):
    shards = (
        norm_gain,
        w_query,
        w_key,
        w_value,
        w_outgate,
        w_lowrank,
        w_rank_up,
        gate_bias,
        head_gain,
        w_output,
        ffn_gain,
        w_gate,
        w_up,
        w_down,
    )
    full = (
        lax.all_gather(shards[0], "shard", axis=0, tiled=True),
        lax.all_gather(shards[1], "shard", axis=0, tiled=True),
        lax.all_gather(shards[2], "shard", axis=0, tiled=True),
        lax.all_gather(shards[3], "shard", axis=0, tiled=True),
        lax.all_gather(shards[4], "shard", axis=0, tiled=True),
        lax.all_gather(shards[5], "shard", axis=0, tiled=True),
        lax.all_gather(shards[6], "shard", axis=0, tiled=True),
        lax.all_gather(shards[7], "shard", axis=0, tiled=True),
        lax.all_gather(shards[8], "shard", axis=0, tiled=True),
        lax.all_gather(shards[9], "shard", axis=0, tiled=True),
        lax.all_gather(shards[10], "shard", axis=0, tiled=True),
        lax.all_gather(shards[11], "shard", axis=0, tiled=True),
        lax.all_gather(shards[12], "shard", axis=0, tiled=True),
        lax.all_gather(shards[13], "shard", axis=0, tiled=True),
    )
    (
        gain_attn,
        query_w,
        key_w,
        value_w,
        outgate_w,
        lowrank_w,
        rank_up_w,
        bias_full,
        head_w,
        output_w,
        gain_ffn,
        gate_w,
        up_w,
        down_w,
    ) = full
    residual_in = tokens.astype(jnp.float32)
    count_of_rows = residual_in.shape[0]
    block_count = count_of_rows // BLOCK
    slice_start = seq_start[0]
    resets = (jnp.arange(block_count, dtype=jnp.int32) * BLOCK == slice_start).astype(jnp.float32)
    gain_one = gain_attn.astype(jnp.float32)
    normed = rms_norm(residual_in, gain_one).astype(jnp.bfloat16)
    query_rows = dense(normed, query_w).astype(jnp.bfloat16)
    key_rows = dense(normed, key_w).astype(jnp.bfloat16)
    rows_of_value = dense(normed, value_w).astype(jnp.bfloat16)
    outgate = dense(normed, outgate_w)
    rank_rows = dense(normed, lowrank_w).astype(jnp.bfloat16)
    gate_logit = dense(rank_rows, rank_up_w) + bias_full.astype(jnp.float32)
    log_decay = jax.nn.log_sigmoid(gate_logit) / normalizer
    query_f = query_rows.astype(jnp.float32)
    key_f = key_rows.astype(jnp.float32)
    value_f = rows_of_value.astype(jnp.float32)
    zero_state = jnp.zeros((HEAD_COUNT, DK, VALUE_WIDTH), jnp.float32)
    local_mixed, local_end = mixer(query_f, key_f, value_f, log_decay, resets, zero_state)
    has_start = slice_start < count_of_rows
    decay_heads = log_decay.reshape(count_of_rows, HEAD_COUNT, DK)
    carry_decay = jnp.where(has_start, 0.0, jnp.exp(jnp.sum(decay_heads, axis=0)))
    identity = (jnp.ones_like(carry_decay), jnp.zeros_like(local_end))
    incoming_state = carried_in((carry_decay, local_end), ("replica", "shard"), link, identity)[1]
    before = (jnp.arange(count_of_rows, dtype=jnp.int32) < slice_start).astype(jnp.float32)
    query_before_decay = (
        query_f.reshape(count_of_rows, HEAD_COUNT, DK)
        * jnp.exp(jnp.cumsum(decay_heads, axis=0))
        * before[:, None, None]
    )
    carried_over = jnp.einsum(
        "pde,dec->pdc", query_before_decay, incoming_state, precision=precise_mode
    )
    mixed_rows = local_mixed + carried_over.reshape(count_of_rows, HEAD_COUNT * VALUE_WIDTH)
    head_one = head_w.astype(jnp.float32)
    gated_rows = output_gate(mixed_rows, outgate, head_one).astype(jnp.bfloat16)
    middle = residual_in + dense(gated_rows, output_w)
    gain_two = gain_ffn.astype(jnp.float32)
    normed_ffn = rms_norm(middle, gain_two).astype(jnp.bfloat16)
    gate_pre = dense(normed_ffn, gate_w)
    up_pre = dense(normed_ffn, up_w)
    hidden = swiglu(gate_pre, up_pre).astype(jnp.bfloat16)
    output = (middle + dense(hidden, down_w)).astype(jnp.bfloat16)
    again = (
        lax.all_gather(shards[0], "shard", axis=0, tiled=True),
        lax.all_gather(shards[1], "shard", axis=0, tiled=True),
        lax.all_gather(shards[2], "shard", axis=0, tiled=True),
        lax.all_gather(shards[3], "shard", axis=0, tiled=True),
        lax.all_gather(shards[4], "shard", axis=0, tiled=True),
        lax.all_gather(shards[5], "shard", axis=0, tiled=True),
        lax.all_gather(shards[6], "shard", axis=0, tiled=True),
        lax.all_gather(shards[7], "shard", axis=0, tiled=True),
        lax.all_gather(shards[8], "shard", axis=0, tiled=True),
        lax.all_gather(shards[9], "shard", axis=0, tiled=True),
        lax.all_gather(shards[10], "shard", axis=0, tiled=True),
        lax.all_gather(shards[11], "shard", axis=0, tiled=True),
        lax.all_gather(shards[12], "shard", axis=0, tiled=True),
        lax.all_gather(shards[13], "shard", axis=0, tiled=True),
    )
    (
        gain_attn,
        query_w,
        key_w,
        value_w,
        outgate_w,
        lowrank_w,
        rank_up_w,
        bias_full,
        head_w,
        output_w,
        gain_ffn,
        gate_w,
        up_w,
        down_w,
    ) = again
    grad_out = out_grad.astype(jnp.float32)
    grad_down = dense_left(hidden, out_grad)
    grad_hidden = dense_back(out_grad, down_w)
    unused, pull_swiglu = jax.vjp(swiglu, gate_pre, up_pre)
    grad_gate_f, grad_up_f = pull_swiglu(grad_hidden)
    grad_gate_rows = grad_gate_f.astype(jnp.bfloat16)
    grad_up_rows = grad_up_f.astype(jnp.bfloat16)
    grad_gate_w = dense_left(normed_ffn, grad_gate_rows)
    grad_up_w = dense_left(normed_ffn, grad_up_rows)
    grad_normed_ffn = dense_back(grad_gate_rows, gate_w) + dense_back(grad_up_rows, up_w)
    unused, pull_norm_two = jax.vjp(rms_norm, middle, gain_two)
    grad_middle_part, grad_gain_two = pull_norm_two(grad_normed_ffn)
    grad_middle = grad_out + grad_middle_part
    grad_attn = grad_middle.astype(jnp.bfloat16)
    grad_output_w = dense_left(gated_rows, grad_attn)
    grad_gated = dense_back(grad_attn, output_w)
    unused, pull_gate = jax.vjp(output_gate, mixed_rows, outgate, head_one)
    mixed_gradient, grad_outgate_f, grad_head = pull_gate(grad_gated)
    grad_outgate = grad_outgate_f.astype(jnp.bfloat16)
    carry_grad = jnp.einsum(
        "fin,fig->ing",
        query_before_decay,
        mixed_gradient.reshape(count_of_rows, HEAD_COUNT, VALUE_WIDTH),
        precision=precise_mode,
    )
    outgoing = entering((carry_decay, carry_grad), ("replica", "shard"), link, identity)[1]

    def local_mixer(query_in, key_in, value_in, decay_in):
        return mixer(query_in, key_in, value_in, decay_in, resets, incoming_state)

    unused, pull_mixer = jax.vjp(local_mixer, query_f, key_f, value_f, log_decay)
    grad_query_f, grad_key_f, grad_value_f, grad_decay = pull_mixer((mixed_gradient, outgoing))
    grad_query = grad_query_f.astype(jnp.bfloat16)
    grad_key = grad_key_f.astype(jnp.bfloat16)
    grad_value = grad_value_f.astype(jnp.bfloat16)
    grad_logit = (grad_decay * jax.nn.sigmoid(-gate_logit) / normalizer).astype(jnp.bfloat16)
    grad_bias = jnp.sum(grad_logit.astype(jnp.float32), axis=0)
    grad_rank_up = dense_left(rank_rows, grad_logit)
    grad_rank = dense_back(grad_logit, rank_up_w).astype(jnp.bfloat16)
    grad_lowrank = dense_left(normed, grad_rank)
    grad_query_w = dense_left(normed, grad_query)
    grad_key_w = dense_left(normed, grad_key)
    grad_value_w = dense_left(normed, grad_value)
    grad_outgate_w = dense_left(normed, grad_outgate)
    grad_normed = (
        dense_back(grad_query, query_w)
        + dense_back(grad_key, key_w)
        + dense_back(grad_value, value_w)
        + dense_back(grad_outgate, outgate_w)
        + dense_back(grad_rank, lowrank_w)
    )
    unused, pull_norm_one = jax.vjp(rms_norm, residual_in, gain_one)
    grad_input_part, grad_gain_one = pull_norm_one(grad_normed)
    grad_tokens = (grad_middle + grad_input_part).astype(jnp.bfloat16)
    gradients = (
        grad_gain_one,
        grad_query_w,
        grad_key_w,
        grad_value_w,
        grad_outgate_w,
        grad_lowrank,
        grad_rank_up,
        grad_bias,
        grad_head,
        grad_output_w,
        grad_gain_two,
        grad_gate_w,
        grad_up_w,
        grad_down,
    )
    summed = (
        lax.psum_scatter(
            gradients[0].astype(jnp.bfloat16), "shard", scatter_dimension=0, tiled=True
        ).astype(jnp.float32),
        lax.psum_scatter(
            gradients[1].astype(jnp.bfloat16), "shard", scatter_dimension=0, tiled=True
        ).astype(jnp.float32),
        lax.psum_scatter(
            gradients[2].astype(jnp.bfloat16), "shard", scatter_dimension=0, tiled=True
        ).astype(jnp.float32),
        lax.psum_scatter(
            gradients[3].astype(jnp.bfloat16), "shard", scatter_dimension=0, tiled=True
        ).astype(jnp.float32),
        lax.psum_scatter(
            gradients[4].astype(jnp.bfloat16), "shard", scatter_dimension=0, tiled=True
        ).astype(jnp.float32),
        lax.psum_scatter(
            gradients[5].astype(jnp.bfloat16), "shard", scatter_dimension=0, tiled=True
        ).astype(jnp.float32),
        lax.psum_scatter(
            gradients[6].astype(jnp.bfloat16), "shard", scatter_dimension=0, tiled=True
        ).astype(jnp.float32),
        lax.psum_scatter(
            gradients[7].astype(jnp.bfloat16), "shard", scatter_dimension=0, tiled=True
        ).astype(jnp.float32),
        lax.psum_scatter(
            gradients[8].astype(jnp.bfloat16), "shard", scatter_dimension=0, tiled=True
        ).astype(jnp.float32),
        lax.psum_scatter(
            gradients[9].astype(jnp.bfloat16), "shard", scatter_dimension=0, tiled=True
        ).astype(jnp.float32),
        lax.psum_scatter(
            gradients[10].astype(jnp.bfloat16), "shard", scatter_dimension=0, tiled=True
        ).astype(jnp.float32),
        lax.psum_scatter(
            gradients[11].astype(jnp.bfloat16), "shard", scatter_dimension=0, tiled=True
        ).astype(jnp.float32),
        lax.psum_scatter(
            gradients[12].astype(jnp.bfloat16), "shard", scatter_dimension=0, tiled=True
        ).astype(jnp.float32),
        lax.psum_scatter(
            gradients[13].astype(jnp.bfloat16), "shard", scatter_dimension=0, tiled=True
        ).astype(jnp.float32),
    )
    totals = lax.psum(
        (
            summed[0],
            summed[1],
            summed[2],
            summed[3],
            summed[4],
            summed[5],
            summed[6],
            summed[7],
            summed[8],
            summed[9],
            summed[10],
            summed[11],
            summed[12],
            summed[13],
        ),
        "replica",
    )
    return (output, grad_tokens) + tuple(totals)


def solution(mesh):
    return jax.shard_map(
        per_device,
        mesh=mesh,
        in_specs=(
            P(("replica", "shard"), None),
            P(("replica", "shard")),
            P(("replica", "shard"), None),
            P("shard"),
            P("shard", None),
            P("shard", None),
            P("shard", None),
            P("shard", None),
            P("shard", None),
            P("shard", None),
            P("shard"),
            P("shard"),
            P("shard", None),
            P("shard"),
            P("shard", None),
            P("shard", None),
            P("shard", None),
        ),
        out_specs=(
            P(("replica", "shard"), None),
            P(("replica", "shard"), None),
            P("shard"),
            P("shard", None),
            P("shard", None),
            P("shard", None),
            P("shard", None),
            P("shard", None),
            P("shard", None),
            P("shard"),
            P("shard"),
            P("shard", None),
            P("shard"),
            P("shard", None),
            P("shard", None),
            P("shard", None),
        ),
        check_vma=False,
    )
```

profile of v0, /device:TPU:0, one launch (start us, length us, event | category | flops | bytes accessed | tf_op | source)
XLA Modules:
  0.0 1663.1 jit_solution(7864951501307224293)
XLA Ops:
  12.4 12.7 all-gather.2
  25.1 13.5 all-gather.3
  38.6 7.6 all-gather.4
  46.2 13.5 all_gather.71
  70.8 3.9 fusion.81
  80.6 3.9 fusion.82
  87.5 29.0 %all-gather.19.cloned.1.call-done = bf16[1024,1024]{1,0:T(8,128)(2,1)} async-done(((bf16[256,1024]{1,0:T(8,128)(2,1)}), bf16[1024,1024]{1,0:T(8,128)(2,1)}) %all-gather.19.cloned.1.call-update) | async-done | bytes 2097168 | tf_op jit(solution)/shard_map/all_gather | solution.py:171
  116.5 6.1 convert_convert_fusion
  122.6 5.6 reshape.297
  128.2 4.8 copy.131
  133.1 116.4 %while.77 = (s32[]{:T(128)}, f32[4,128,256]{2,1,0:T(8,128)S(1)}, f32[16,64,4,256]{3,1,0,2:T(8,128)}, f32[16,64,4,128]{3,2,1,0:T(4,128)}, f32[16]{0:T(128)S(1)}, ...) while((s32[]{:T(128)}, f32[4,128,256]{2,1,0:T(8,128)S(1)}, ...), condition=%wide.region_3.4_spmd.clone, body=%wide.region_1.3_spmd.clone.sunk | while | flops 141516800 | bytes 4635288 | solution.py:124
  253.7 66.7 %all_gather.77 = bf16[32,4,128]{2,1,0:T(4,128)(2,1)S(1)} all-gather(bf16[1,4,128]{2,1,0:T(4,128)(2,1)S(1)} %fusion.101), channel_id=1, replica_groups=mesh['replica'=8,'shard'=4] {'replica','shard'}, dimensions={0}, use_global_device_ids=true | all-gather | bytes 33792 | tf_op jit(solution)/shard_map/all_gather | solution.py:20
  333.6 9.1 all-reduce.1
  342.7 10.5 all-gather.5
  353.2 3.9 copy.140
  363.9 5.4 copy.138
  369.9 5.2 multiply_reduce_fusion.6
  379.7 8.7 fusion.74
  388.5 29.5 %all-gather.25.cloned.1.call-done = bf16[1024,1024]{1,0:T(8,128)(2,1)} async-done(((bf16[256,1024]{1,0:T(8,128)(2,1)}), bf16[1024,1024]{1,0:T(8,128)(2,1)}) %all-gather.25.cloned.1.call-update) | async-done | bytes 2097168 | tf_op jit(solution)/shard_map/all_gather | solution.py:177
  418.0 4.8 multiply_reduce_fusion.5
  426.5 98.6 %all-gather.27.cloned.1.call-done = bf16[1024,2816]{1,0:T(8,128)(2,1)} async-done(((bf16[256,2816]{1,0:T(8,128)(2,1)}), bf16[1024,2816]{1,0:T(8,128)(2,1)}) %all-gather.27.cloned.1.call-update) | async-done | bytes 5767184 | tf_op jit(solution)/shard_map/all_gather | solution.py:179
  525.1 12.1 fusion.118
  537.2 94.5 %all-gather.29.cloned.1.call-done = bf16[1024,2816]{1,0:T(8,128)(2,1)} async-done(((bf16[256,2816]{1,0:T(8,128)(2,1)}), bf16[1024,2816]{1,0:T(8,128)(2,1)}) %all-gather.29.cloned.1.call-update) | async-done | bytes 5767184 | tf_op jit(solution)/shard_map/all_gather | solution.py:180
  631.7 11.9 fusion.119
  643.5 94.7 %all-gather.31.cloned.1.call-done = bf16[2816,1024]{1,0:T(8,128)(2,1)} async-done(((bf16[704,1024]{1,0:T(8,128)(2,1)}), bf16[2816,1024]{1,0:T(8,128)(2,1)}) %all-gather.31.cloned.1.call-update) | async-done | bytes 5767184 | tf_op jit(solution)/shard_map/all_gather | solution.py:181
  738.2 21.4 %multiply_convert_fusion = (bf16[1024,2816]{1,0:T(8,128)(2,1)}, bf16[1024,2816]{1,0:T(8,128)(2,1)}, bf16[1024,2816]{1,0:T(8,128)(2,1)}) fusion(f32[1024,2816]{1,0:T(8,128)} %fusion.118, f32[1024,2816]{1,0:T(8,128)} %fusion.119, bf16[1024,1024]{1,0:T(8,128)(2,1)} %param.29, bf16[2816,1024]{1,0:T(8,128)(2,1)} %all-gather.31.cloned.1.call-done), kind=kOutput, calls=%fused_computation.103 | convolution fusion | flops 5951717376 | bytes 48234496 | tf_op jit(solution)/shard_map/dot_general | solution.py:67
  759.7 10.2 fusion.120
  769.9 9.5 multiply_reduce_fusion.1
  783.8 6.6 fusion.96
  799.2 6.6 convolution_convert_fusion.3
  805.8 5.3 convolution_convert_fusion.4
  811.2 10.9 convolution_convert_fusion.2
  823.7 10.5 convolution_convert_fusion.1
  835.3 88.3 %while.75 = (s32[]{:T(128)}, f32[4,128,256]{2,1,0:T(8,128)S(1)}, f32[16,4,128,256]{3,2,1,0:T(8,128)}, f32[16,64,4,128]{3,2,1,0:T(4,128)}, f32[16]{0:T(128)S(1)},...) while((s32[]{:T(128)}, f32[4,128,256]{2,1,0:T(8,128)S(1)}, ...), condition=%wide.region_17.18_spmd, body=%wide.region_15.17_spmd.sunk | while | flops 52854784 | bytes 3160185 | solution.py:124
  923.6 5.6 copy.146
  929.2 10.7 convolution_convert_fusion
  940.0 56.5 %while.74 = (s32[]{:T(128)}, f32[4,128,256]{2,1,0:T(8,128)S(1)}, s32[]{:T(128)}, bf16[32,4,128]{2,1,0:T(4,128)(2,1)}, bf16[32,4,128,256]{3,2,1,0:T(8,128)(2,1)},...) while((s32[]{:T(128)}, f32[4,128,256]{2,1,0:T(8,128)S(1)}, s32[]{:T(128)}, ...), condition=%wide.region_14.15_spmd, body=%wide.region_13.14_spmd.sunk | while | flops 393734 | bytes 1315987 | solution.py:59
  1001.4 190.6 %while.76 = (s32[]{:T(128)}, f32[4,128,256]{2,1,0:T(8,128)S(1)}, bf16[16,64,4,128]{3,1,2,0:T(8,128)(2,1)S(1)}, bf16[16,64,4,128]{3,1,2,0:T(8,128)(2,1)}, bf16[16...) while((s32[]{:T(128)}, f32[4,128,256]{2,1,0:T(8,128)S(1)}, ...), condition=%wide.region_23.24_spmd, body=%wide.region_18.23_spmd.sunk | while | flops 295641088 | bytes 14631141 | solution.py:124
  1214.0 11.6 add_convert_fusion
  1225.6 4.2 copy.161
  1238.7 6.6 fusion.122
  1245.3 32.3 %reduce-scatter.26.cloned.1.call-done = bf16[704,1024]{1,0:T(8,128)(2,1)} async-done(((bf16[2816,1024]{1,0:T(8,128)(2,1)}), bf16[704,1024]{1,0:T(8,128)(2,1)}) %reduce-scatter.26.cloned.1.call-update) | async-done | bytes 1441808 | tf_op jit(solution)/shard_map/reduce_scatter | solution.py:384
  1290.3 4.1 copy.162
  1294.7 18.7 %all-reduce.8 = (bf16[1024]{0:T(1024)(128)(2,1)S(1)}, bf16[16,512]{1,0:T(8,128)(2,1)S(1)}, bf16[512]{0:T(512)(128)(2,1)S(1)}, bf16[256]{0:T(256)(128)(2,1)S(1)}, bf16[1024]{0:T(1024)(128)(2,1)S(1)}) all-reduce(bf16[1024]{0:T(1024)(128)(2,1)S(1)} %get-tuple-element.660, ...), channel_id=4, replica_groups=mesh['replica'=8,'shard'=4] {'shard'}, use_global_device_ids=true, to_apply=%region_26.27.clone | all-reduce | flops 11008 | bytes 44032
  1313.7 14.7 reduce-scatter.10.cloned.1.call-done
  1328.4 28.6 %reduce-scatter.12.cloned.1.call-done = bf16[256,512]{1,0:T(8,128)(2,1)} async-done(((bf16[1024,512]{1,0:T(8,128)(2,1)}), bf16[256,512]{1,0:T(8,128)(2,1)}) %reduce-scatter.12.cloned.1.call-update) | async-done | bytes 262160 | tf_op jit(solution)/shard_map/reduce_scatter | solution.py:351
  1357.0 45.0 %reduce-scatter.14.cloned.1.call-done = bf16[256,1024]{1,0:T(8,128)(2,1)} async-done(((bf16[1024,1024]{1,0:T(8,128)(2,1)}), bf16[256,1024]{1,0:T(8,128)(2,1)}) %reduce-scatter.14.cloned.1.call-update) | async-done | bytes 524304 | tf_op jit(solution)/shard_map/reduce_scatter | solution.py:354
  1402.1 253.9 %all-reduce.10 = (f32[256]{0:T(256)}, f32[256,512]{1,0:T(8,128)}, f32[256,512]{1,0:T(8,128)}, f32[256,1024]{1,0:T(8,128)}, f32[256,1024]{1,0:T(8,128)}, /*index=...) all-reduce(f32[256]{0:T(256)S(1)} %get-tuple-element.790, ...), channel_id=1, replica_groups=mesh['replica'=8,'shard'=4] {'replica'}, use_global_device_ids=true, to_apply=%region_27.28 | all-reduce | flops 3218112 | bytes 19314176 | tf_op jit(solution)/shard_map/psum | solution.py:388
  (972 shorter events, 534.9 us)
Async XLA Ops:
  7.2 5.2 copy-start.44
  7.2 17.9 %copy-start.37 = (bf16[4,512]{1,0:T(4,128)(2,1)S(1)}, bf16[4,512]{1,0:T(4,128)(2,1)}, u32[]{:S(2)}) copy-start(bf16[4,512]{1,0:T(4,128)(2,1)} %param.36) | copy-start | bytes 12292
  7.2 31.4 %copy-start.40 = (bf16[128]{0:T(256)(128)(2,1)S(1)}, bf16[128]{0:T(256)(128)(2,1)}, u32[]{:S(2)}) copy-start(bf16[128]{0:T(256)(128)(2,1)} %param.37) | copy-start | bytes 772
  7.2 39.0 %copy-start.36 = (bf16[256,16]{0,1:T(8,128)(2,1)S(1)}, bf16[256,16]{0,1:T(8,128)(2,1)}, u32[]{:S(2)}) copy-start(bf16[256,16]{0,1:T(8,128)(2,1)} %param.35) | copy-start | bytes 24580
  7.2 63.6 %all-gather.21.cloned.1.call-start = ((), (), s32[]{:S(2)}) async-start(), calls=%async_computation.11 | async-start | bytes 1310720 | tf_op jit(solution)/shard_map/all_gather | solution.py:169
  8.0 72.7 %all-gather.17.cloned.1.call-start = ((), (), s32[]{:S(2)}) async-start(), calls=%async_computation.9 | async-start | bytes 1310720 | tf_op jit(solution)/shard_map/all_gather | solution.py:170
  8.7 107.8 %all-gather.19.cloned.1.call-start = ((), (), s32[]{:S(2)}) async-start(), calls=%async_computation.10 | async-start | bytes 2621440 | tf_op jit(solution)/shard_map/all_gather | solution.py:171
  9.4 359.8 %all-gather.33.cloned.1.call-start = ((), (), s32[]{:S(2)}) async-start(), calls=%async_computation.26 | async-start | bytes 8650752 | tf_op jit(solution)/shard_map/all_gather | solution.py:20
  12.4 793.4 %copy-start.5 = (bf16[1024,1024]{0,1:T(8,128)(2,1)}, bf16[1024,1024]{0,1:T(8,128)(2,1)S(1)}, u32[]{:S(2)}) copy-start(bf16[1024,1024]{0,1:T(8,128)(2,1)S(1)} %copy.128) | copy-start | bytes 6291460
  38.6 25.7 %copy-start.27 = (bf16[16,512]{1,0:T(8,128)(2,1)}, bf16[16,512]{1,0:T(8,128)(2,1)S(1)}, u32[]{:S(2)}) copy-start(bf16[16,512]{1,0:T(8,128)(2,1)S(1)} %reshape.306) | copy-start | bytes 49156
  46.2 18.1 %copy-start.34 = (f32[4,1,128]{2,1,0:T(1,128)}, f32[4,1,128]{2,1,0:T(1,128)S(1)}, u32[]{:S(2)}) copy-start(f32[4,1,128]{2,1,0:T(1,128)S(1)} %convert_element_type.311) | copy-start | bytes 6148
  59.7 4.6 copy-start.25
  60.2 4.1 copy-start.30
  60.8 6.4 copy-start.32
  249.5 73.8 %copy-start.47 = (f32[16]{0:T(128)}, f32[16]{0:T(128)S(1)}, u32[]{:S(2)}) copy-start(f32[16]{0:T(128)S(1)} %get-tuple-element.1300) | copy-start | bytes 196
  250.3 129.5 %all-gather.23.cloned.1.call-start = ((), (), s32[]{:S(2)}) async-start(), calls=%async_computation.12 | async-start | bytes 2621440 | tf_op jit(solution)/shard_map/all_gather | solution.py:172
  250.9 167.2 %all-gather.25.cloned.1.call-start = ((), (), s32[]{:S(2)}) async-start(), calls=%async_computation.13 | async-start | bytes 2621440 | tf_op jit(solution)/shard_map/all_gather | solution.py:177
  251.4 273.7 %all-gather.27.cloned.1.call-start = ((), (), s32[]{:S(2)}) async-start(), calls=%async_computation.14 | async-start | bytes 7208960 | tf_op jit(solution)/shard_map/all_gather | solution.py:179
  252.2 379.5 %all-gather.29.cloned.1.call-start = ((), (), s32[]{:S(2)}) async-start(), calls=%async_computation.15 | async-start | bytes 7208960 | tf_op jit(solution)/shard_map/all_gather | solution.py:180
  252.9 485.3 %all-gather.31.cloned.1.call-start = ((), (), s32[]{:S(2)}) async-start(), calls=%async_computation.16 | async-start | bytes 7208960 | tf_op jit(solution)/shard_map/all_gather | solution.py:181
  253.7 686.3 %all-gather.35.cloned.1.call-start = ((), (), s32[]{:S(2)}) async-start(), calls=%async_computation.27 | async-start | bytes 8650752 | tf_op jit(solution)/shard_map/all_gather | solution.py:42
  327.6 4.5 copy-start.38
  327.7 5.7 copy-start.45
  327.7 15.0 copy-start.46
  369.9 5.2 copy-start
  759.7 10.3 copy-start.11
  759.7 10.3 copy-start.41
  769.9 9.5 copy-start.13
  779.5 4.4 copy-start.43
  780.5 9.9 copy-start.8
  783.8 6.6 copy-start.3
  798.7 446.6 %reduce-scatter.20.cloned.1.call-start = ((), (), s32[]{:S(2)}) async-start(), calls=%async_computation.22 | async-start | bytes 2621440 | tf_op jit(solution)/shard_map/reduce_scatter | solution.py:372
  805.8 439.5 %reduce-scatter.16.cloned.1.call-start = ((), (), s32[]{:S(2)}) async-start(), calls=%async_computation.20 | async-start | bytes 2621440 | tf_op jit(solution)/shard_map/reduce_scatter | solution.py:357
  811.2 434.1 %reduce-scatter.22.cloned.1.call-start = ((), (), s32[]{:S(2)}) async-start(), calls=%async_computation.23 | async-start | bytes 7208960 | tf_op jit(solution)/shard_map/reduce_scatter | solution.py:378
  822.2 423.1 %reduce-scatter.24.cloned.1.call-start = ((), (), s32[]{:S(2)}) async-start(), calls=%async_computation.24 | async-start | bytes 7208960 | tf_op jit(solution)/shard_map/reduce_scatter | solution.py:381
  834.2 443.4 %reduce-scatter.26.cloned.1.call-start = ((), (), s32[]{:S(2)}) async-start(), calls=%async_computation.25 | async-start | bytes 7208960 | tf_op jit(solution)/shard_map/reduce_scatter | solution.py:384
  923.6 5.6 copy-start.18
  939.9 373.8 %reduce-scatter.18.cloned.1.call-start = ((), (), s32[]{:S(2)}) async-start(), calls=%async_computation.21 | async-start | bytes 40960 | tf_op jit(solution)/shard_map/reduce_scatter | solution.py:360
  1193.8 3.7 copy-start.35
  1195.6 4.9 copy-start.28
  1195.6 5.2 copy-start.6
  1202.2 126.2 %reduce-scatter.10.cloned.1.call-start = ((), (), s32[]{:S(2)}) async-start(), calls=%async_computation.17 | async-start | bytes 1310720 | tf_op jit(solution)/shard_map/reduce_scatter | solution.py:348
  1206.0 151.1 %reduce-scatter.12.cloned.1.call-start = ((), (), s32[]{:S(2)}) async-start(), calls=%async_computation.18 | async-start | bytes 1310720 | tf_op jit(solution)/shard_map/reduce_scatter | solution.py:351
  1214.0 188.1 %reduce-scatter.14.cloned.1.call-start = ((), (), s32[]{:S(2)}) async-start(), calls=%async_computation.19 | async-start | bytes 2621440 | tf_op jit(solution)/shard_map/reduce_scatter | solution.py:354
  1290.3 4.1 copy-start.33
  1290.3 4.5 copy-start.39
  1290.3 111.8 %copy-start.22 = (bf16[256,2816]{1,0:T(8,128)(2,1)S(1)}, bf16[256,2816]{1,0:T(8,128)(2,1)}, u32[]{:S(2)}) copy-start(bf16[256,2816]{1,0:T(8,128)(2,1)} %reduce-scatter.22.cloned.1.call-done) | copy-start | bytes 4325380
  1290.3 111.8 %copy-start.24 = (bf16[256,1024]{1,0:T(8,128)(2,1)S(1)}, bf16[256,1024]{1,0:T(8,128)(2,1)}, u32[]{:S(2)}) copy-start(bf16[256,1024]{1,0:T(8,128)(2,1)} %reduce-scatter.20.cloned.1.call-done) | copy-start | bytes 1572868
  (20 other events, 39.3 us)
Sparse Core Ops, SparseCore 0:
  9.6 30.9 all-gather.20
  42.2 27.5 all-gather.16
  71.3 45.1 all-gather.18
  250.4 75.8 all-gather.32
  327.7 44.4 all-gather.22
  373.7 44.3 all-gather.24
  419.6 105.4 all-gather.26
  526.7 104.9 all-gather.28
  633.2 104.9 all-gather.30
  798.8 75.3 all-gather.34
  876.5 42.2 reduce-scatter.19
  921.0 42.8 reduce-scatter.15
  966.1 101.4 reduce-scatter.21
  1069.8 102.7 reduce-scatter.23
  1174.8 102.7 reduce-scatter.25
  1280.3 19.7 reduce-scatter.17
  1302.8 25.5 reduce-scatter.9
  1331.1 25.8 reduce-scatter.11
  1359.9 42.1 reduce-scatter.13
where the time goes:
time: 1680 us; the launch traced here: 1660 us
  waiting for transfers between devices  472 us (28%)
  blocking collectives  406 us (24%)
  matrix products  347 us (21%)
  local copies, waits for them, and re-layouts  216 us (13%)
  other arithmetic  165 us (10%)
  loops' own time  35.8 us (2%)
  between operations  19.1 us (1%)
    psum x1, blocking collectives, per_device(): lax.psum((summed[0], summed[1], summed[2], summed[3], summed[4], summed[5...  254 us
    all_gather x1, waiting for transfers between devices, per_device(): lax.all_gather(shards[11], 'shard', axis=0, tiled=True)  98.6 us
    all_gather x1, waiting for transfers between devices, per_device(): lax.all_gather(shards[13], 'shard', axis=0, tiled=True)  94.7 us
    all_gather x1, waiting for transfers between devices, per_device(): lax.all_gather(shards[12], 'shard', axis=0, tiled=True)  94.5 us
    dot_general x10, matrix products, dense(): return jnp.dot(left, right, preferred_element_type=jnp.float32)  67.1 us
    all_gather x1, blocking collectives, carried_in(): lax.all_gather(a.astype(kind), axis)  66.7 us
    squeeze x64, local copies, waits for them, and re-layouts, mixer(): lax.scan(jax.checkpoint(block_step), entering_state, shaped)  63.7 us
    dot_general x10, matrix products, dense_back(): lax.dot_general(grad_rows, weight, (((1,), (1,)), ((), ())), preferred_el...  63.4 us
  transfers between devices with their start and end apart: 19, of which 9 were waited for; matrix products, arithmetic and copies ran while one was open for 32% of the time, Pallas kernels for 0%

commit v1 on v0

v1 whole, which is shorter than its diff:
```python
import jax
import jax.numpy as jnp
from jax import lax
from jax.experimental import pallas as pl
from jax.experimental.pallas import tpu as pltpu
from jax.sharding import PartitionSpec as P

HEAD_COUNT = 4
DK = 128
VALUE_WIDTH = 256
BLOCK = 64
KD = HEAD_COUNT * DK
VD = HEAD_COUNT * VALUE_WIDTH
EVERY = ("replica", "shard")
ROWS = ("shard", "replica")
SIDE = 128

epsilon = 1e-05
normalizer = 16.0
highest = lax.Precision.HIGHEST
high = lax.Precision.HIGH


def dense(left, right):
    return jnp.dot(left, right, preferred_element_type=jnp.float32)


def dense_back(grad_rows, weight):
    return lax.dot_general(
        grad_rows, weight, (((1,), (1,)), ((), ())), preferred_element_type=jnp.float32
    )


def dense_left(input_rows, grad_rows):
    return lax.dot_general(
        input_rows, grad_rows, (((0,), (0,)), ((), ())), preferred_element_type=jnp.float32
    )


def rms_norm(values, gain):
    return values * lax.rsqrt(jnp.mean(values * values, axis=-1, keepdims=True) + epsilon) * gain


def output_gate(mixed_rows, outgate, head_gain):
    count_of_rows = mixed_rows.shape[0]
    shaped = rms_norm(
        mixed_rows.reshape(count_of_rows, HEAD_COUNT, VALUE_WIDTH), head_gain
    ).reshape(count_of_rows, HEAD_COUNT * VALUE_WIDTH)
    return shaped * jax.nn.silu(outgate)


def swiglu(gate_pre, up_pre):
    return jax.nn.silu(gate_pre) * up_pre


def halves(a):
    if a.dtype == jnp.bfloat16:
        return (a, None)
    top = a.astype(jnp.bfloat16)
    return (top, (a - top.astype(jnp.float32)).astype(jnp.bfloat16))


def product(left, right, dims):
    def one(a, b):
        return lax.dot_general(a, b, (dims, ((), ())), preferred_element_type=jnp.float32)

    total = one(left[0], right[0])
    if left[1] is not None:
        total = total + one(left[1], right[0])
    if right[1] is not None:
        total = total + one(left[0], right[1])
    return total


def exact(left, right):
    return lax.dot_general(
        left, right, (NT, ((), ())), precision=highest, preferred_element_type=jnp.float32
    )


NN = ((1,), (0,))
NT = ((1,), (1,))
TN = ((0,), (0,))


def causal_mask():
    rows = lax.broadcasted_iota(jnp.int32, (BLOCK, BLOCK), 0)
    cols = lax.broadcasted_iota(jnp.int32, (BLOCK, BLOCK), 1)
    return rows >= cols


def forward_kernel(start_ref, qkv_ref, cumul_ref, incoming_ref, mixed_ref, saved_ref, state_ref):
    block = pl.program_id(0)

    @pl.when(block == 0)
    def _():
        state_ref[...] = incoming_ref[...].astype(jnp.float32)

    keep = jnp.where(block * BLOCK == start_ref[0], 0.0, 1.0)
    causal = causal_mask()
    for h in range(HEAD_COUNT):
        ks = slice(h * DK, (h + 1) * DK)
        vs = slice(h * VALUE_WIDTH, (h + 1) * VALUE_WIDTH)
        query = qkv_ref[:, ks].astype(jnp.float32)
        key = qkv_ref[:, KD + h * DK : KD + (h + 1) * DK].astype(jnp.float32)
        value = qkv_ref[:, 2 * KD + h * VALUE_WIDTH : 2 * KD + (h + 1) * VALUE_WIDTH]
        cumul = cumul_ref[:, ks]
        stop = cumul[BLOCK - 1 :, :]
        state = state_ref[vs, :] * keep
        saved_ref[0, vs, :] = state
        query_f = query * jnp.exp(cumul)
        key_f = key * jnp.exp(-cumul)
        query_dec = halves(query_f)
        key_end = halves(key * jnp.exp(stop - cumul))
        scores = jnp.where(causal, exact(query_f, key_f), 0.0)
        mixed_ref[:, vs] = product(query_dec, halves(state), NT) + product(
            halves(scores), (value, None), NN
        )
        state_ref[vs, :] = state * jnp.exp(stop) + product((value, None), key_end, TN)


def backward_kernel(
    start_ref, qkv_ref, cumul_ref, grad_ref, saved_ref, outgoing_ref, gqkv_ref, gdecay_ref, back_ref
):
    step = pl.program_id(0)
    block = pl.num_programs(0) - 1 - step

    @pl.when(step == 0)
    def _():
        back_ref[...] = outgoing_ref[...].astype(jnp.float32)

    keep = jnp.where(block * BLOCK == start_ref[0], 0.0, 1.0)
    causal = causal_mask()
    suffix = jnp.where(
        lax.broadcasted_iota(jnp.int32, (BLOCK, BLOCK), 0)
        <= lax.broadcasted_iota(jnp.int32, (BLOCK, BLOCK), 1),
        1.0,
        0.0,
    )
    last = lax.broadcasted_iota(jnp.int32, (BLOCK, DK), 0) == BLOCK - 1
    for h in range(HEAD_COUNT):
        ks = slice(h * DK, (h + 1) * DK)
        ks2 = slice(KD + h * DK, KD + (h + 1) * DK)
        vs = slice(h * VALUE_WIDTH, (h + 1) * VALUE_WIDTH)
        vs2 = slice(2 * KD + h * VALUE_WIDTH, 2 * KD + (h + 1) * VALUE_WIDTH)
        query = qkv_ref[:, ks].astype(jnp.float32)
        key = qkv_ref[:, ks2].astype(jnp.float32)
        value = (qkv_ref[:, vs2], None)
        cumul = cumul_ref[:, ks]
        stop = cumul[BLOCK - 1 :, :]
        grow = jnp.exp(cumul)
        shrink = jnp.exp(-cumul)
        to_end = jnp.exp(stop - cumul)
        whole = jnp.exp(stop)
        query_f = query * grow
        key_f = key * shrink
        end_f = key * to_end
        query_dec = halves(query_f)
        key_dec = halves(key_f)
        key_end = halves(end_f)
        grad_f = grad_ref[:, vs]
        grad = halves(grad_f)
        rest = (grad_f - grad[0].astype(jnp.float32)) - grad[1].astype(jnp.float32)
        grad_value = product(grad, value, NT) + product(
            (rest.astype(jnp.bfloat16), None), value, NT
        )
        state_f = saved_ref[0, vs, :]
        back_f = back_ref[vs, :]
        state = halves(state_f)
        back = halves(back_f)
        scores = halves(jnp.where(causal, product(query_dec, key_dec, NT), 0.0))
        pull = halves(jnp.where(causal, grad_value, 0.0))
        g_query_dec = product(grad, state, NN) + product(pull, key_dec, NN)
        g_key_dec = product(pull, query_dec, TN)
        g_key_end = product(value, back, NN)
        g_value = product(scores, grad, TN) + product(key_end, back, NT)
        gqkv_ref[:, ks] = (g_query_dec * grow).astype(jnp.bfloat16)
        gqkv_ref[:, ks2] = (g_key_dec * shrink + g_key_end * to_end).astype(jnp.bfloat16)
        gqkv_ref[:, vs2] = g_value.astype(jnp.bfloat16)
        end_part = g_key_end * end_f
        at_stop = jnp.sum(end_part, axis=0, keepdims=True) + whole * jnp.sum(
            state_f * back_f, axis=0, keepdims=True
        )
        g_cumul = g_query_dec * query_f - g_key_dec * key_f - end_part
        g_cumul = g_cumul + jnp.where(last, at_stop, 0.0)
        gdecay_ref[:, ks] = lax.dot_general(
            suffix, g_cumul, (NN, ((), ())), precision=highest, preferred_element_type=jnp.float32
        )
        back_ref[vs, :] = (back_f * whole + product(grad, query_dec, TN)) * keep


def rows_spec(width, index):
    return pl.BlockSpec((BLOCK, width), index)


def mix_forward(start, qkv, cumul, incoming):
    count = qkv.shape[0] // BLOCK
    place = lambda i, s: (i, 0)
    return pl.pallas_call(
        forward_kernel,
        grid_spec=pltpu.PrefetchScalarGridSpec(
            num_scalar_prefetch=1,
            grid=(count,),
            in_specs=[
                rows_spec(2 * KD + VD, place),
                rows_spec(KD, place),
                pl.BlockSpec((VD, DK), lambda i, s: (0, 0)),
            ],
            out_specs=[
                rows_spec(VD, place),
                pl.BlockSpec((1, VD, DK), lambda i, s: (i, 0, 0)),
            ],
            scratch_shapes=[pltpu.VMEM((VD, DK), jnp.float32)],
        ),
        out_shape=[
            jax.ShapeDtypeStruct((count * BLOCK, VD), jnp.float32),
            jax.ShapeDtypeStruct((count, VD, DK), jnp.float32),
        ],
        name="mix_forward",
    )(start, qkv, cumul, incoming)


def mix_backward(start, qkv, cumul, grad, saved, outgoing):
    count = qkv.shape[0] // BLOCK
    place = lambda i, s: (count - 1 - i, 0)
    return pl.pallas_call(
        backward_kernel,
        grid_spec=pltpu.PrefetchScalarGridSpec(
            num_scalar_prefetch=1,
            grid=(count,),
            in_specs=[
                rows_spec(2 * KD + VD, place),
                rows_spec(KD, place),
                rows_spec(VD, place),
                pl.BlockSpec((1, VD, DK), lambda i, s: (count - 1 - i, 0, 0)),
                pl.BlockSpec((VD, DK), lambda i, s: (0, 0)),
            ],
            out_specs=[
                rows_spec(2 * KD + VD, place),
                rows_spec(KD, place),
            ],
            scratch_shapes=[pltpu.VMEM((VD, DK), jnp.float32)],
        ),
        out_shape=[
            jax.ShapeDtypeStruct((count * BLOCK, 2 * KD + VD), jnp.bfloat16),
            jax.ShapeDtypeStruct((count * BLOCK, KD), jnp.float32),
        ],
        name="mix_backward",
    )(start, qkv, cumul, grad, saved, outgoing)


def chain(pieces, decays, reverse):
    count = pieces.shape[0]

    def kernel(pieces_ref, decays_ref, out_ref):
        def one(step, state):
            at = count - 1 - step if reverse else step
            out_ref[at] = state.astype(jnp.bfloat16)
            return decays_ref[at] * state + pieces_ref[at].astype(jnp.float32)

        lax.fori_loop(0, count, one, jnp.zeros(pieces.shape[1:], jnp.float32))

    return pl.pallas_call(
        kernel,
        out_shape=jax.ShapeDtypeStruct(pieces.shape, jnp.bfloat16),
        name="chain_back" if reverse else "chain",
    )(pieces, decays)


def exchange(state, decay_all, reverse):
    count = decay_all.shape[0]
    rows = VD // count
    mine = lax.axis_index(EVERY)
    head = mine * rows // VALUE_WIDTH
    pieces = lax.all_to_all(state.astype(jnp.bfloat16).reshape(count, rows, DK), EVERY, 0, 0)
    decays = lax.dynamic_slice_in_dim(decay_all, head * DK, DK, 1)[:, None, :]
    folded = chain(pieces, decays, reverse)
    return lax.all_to_all(folded, EVERY, 0, 0).reshape(VD, DK)


def fetch(shard):
    piece = shard.shape[0] // lax.axis_size("replica")
    mine = lax.dynamic_slice_in_dim(shard, lax.axis_index("replica") * piece, piece, 0)
    return lax.all_gather(mine, ROWS, axis=0, tiled=True)


def reduce_rows(term):
    return lax.psum_scatter(term.astype(jnp.bfloat16), ROWS, scatter_dimension=0, tiled=True)


def gather_rows(part):
    return lax.all_gather(part, "replica", axis=0, tiled=True)


def column(vector, rows):
    return jnp.pad(vector, (0, rows - vector.shape[0]))[:, None]


def per_device(
    tokens,
    seq_start,
    out_grad,
    norm_gain,
    w_query,
    w_key,
    w_value,
    w_outgate,
    w_lowrank,
    w_rank_up,
    gate_bias,
    head_gain,
    w_output,
    ffn_gain,
    w_gate,
    w_up,
    w_down,
):
    shards = lax.axis_size("shard")
    rows = w_query.shape[0]
    rank = w_lowrank.shape[1]
    spread = w_rank_up.size // rows
    at_norm = rank
    at_ffn = rank + 1
    at_bias = rank + 2
    at_head = rank + 3
    at_up = rank + 4
    side = jnp.concatenate(
        [
            w_lowrank,
            norm_gain[:, None],
            ffn_gain[:, None],
            column(gate_bias, rows),
            column(head_gain, rows),
            w_rank_up.reshape(rows, spread),
            jnp.zeros((rows, SIDE - at_up - spread), jnp.bfloat16),
        ],
        axis=1,
    )
    mixer_w = fetch(jnp.concatenate([w_query, w_key, w_value, w_outgate, side], axis=1))
    output_w = fetch(w_output)
    gate_up_w = fetch(jnp.concatenate([w_gate, w_up], axis=1))
    down_w = fetch(w_down)

    qkv_width = 2 * KD + VD
    wide = qkv_width + VD
    side_w = mixer_w[:, wide:]
    lowrank_w = side_w[:, :rank]
    gain_one = side_w[:, at_norm].astype(jnp.float32)
    gain_two = side_w[:, at_ffn].astype(jnp.float32)
    bias_full = side_w[:, at_bias].reshape(shards, rows)[:, : gate_bias.shape[0]].reshape(-1)
    head_one = (
        side_w[:, at_head].reshape(shards, rows)[:, : head_gain.shape[0]].reshape(-1)
    ).astype(jnp.float32)
    rank_up_w = side_w[:, at_up : at_up + spread].reshape(rank, KD)

    residual_in = tokens.astype(jnp.float32)
    count_of_rows = residual_in.shape[0]
    block_count = count_of_rows // BLOCK
    slice_start = seq_start[0]
    normed = rms_norm(residual_in, gain_one).astype(jnp.bfloat16)
    qkv = dense(normed, mixer_w[:, :qkv_width]).astype(jnp.bfloat16)
    outgate = dense(normed, mixer_w[:, qkv_width:wide])
    rank_rows = dense(normed, lowrank_w).astype(jnp.bfloat16)
    gate_logit = dense(rank_rows, rank_up_w) + bias_full.astype(jnp.float32)
    log_decay = jax.nn.log_sigmoid(gate_logit) / normalizer

    lower = jnp.tril(jnp.ones((BLOCK, BLOCK), jnp.float32))
    cumul3 = jnp.einsum(
        "ij,bjk->bik", lower, log_decay.reshape(block_count, BLOCK, KD), precision=highest
    )
    stops = cumul3[:, -1]
    strict = jnp.tril(jnp.ones((block_count, block_count), jnp.float32), -1)
    ahead_of = jnp.dot(strict, stops, precision=highest)
    after = jnp.dot(strict.T, stops, precision=highest)
    cumul = cumul3.reshape(count_of_rows, KD)
    query_f = qkv[:, :KD].astype(jnp.float32)
    key_f = qkv[:, KD : 2 * KD].astype(jnp.float32)
    value_rows = qkv[:, 2 * KD :]
    has_start = slice_start < count_of_rows
    at = jnp.arange(count_of_rows, dtype=jnp.int32)[:, None]
    to_end = jnp.exp((stops + after)[:, None, :] - cumul3).reshape(count_of_rows, KD)
    counts = jnp.logical_or(jnp.logical_not(has_start), at >= slice_start)
    key_to_end = jnp.where(counts, key_f * to_end, 0.0)
    from_first = jnp.exp(ahead_of[:, None, :] + cumul3).reshape(count_of_rows, KD)
    query_first = jnp.where(at < slice_start, query_f * from_first, 0.0)
    carry_decay = jnp.where(has_start, 0.0, jnp.exp(jnp.sum(stops, axis=0)))
    decay_all = lax.all_gather(carry_decay, EVERY)

    def heads(rows_of, width):
        return rows_of.reshape(count_of_rows, HEAD_COUNT, width)

    local_end = jnp.einsum(
        "thv,thk->hvk",
        heads(value_rows.astype(jnp.float32), VALUE_WIDTH),
        heads(key_to_end, DK),
        precision=high,
    ).reshape(VD, DK)
    incoming = exchange(local_end, decay_all, False)
    mixed_rows, saved = mix_forward(seq_start, qkv, cumul, incoming)
    gated_rows = output_gate(mixed_rows, outgate, head_one).astype(jnp.bfloat16)
    middle = residual_in + dense(gated_rows, output_w)
    normed_ffn = rms_norm(middle, gain_two).astype(jnp.bfloat16)
    width = w_gate.shape[1]
    gate_w = gate_up_w[:, :width]
    up_w = gate_up_w[:, width:]
    gate_pre = dense(normed_ffn, gate_w)
    up_pre = dense(normed_ffn, up_w)
    hidden = swiglu(gate_pre, up_pre).astype(jnp.bfloat16)
    output = (middle + dense(hidden, down_w)).astype(jnp.bfloat16)

    grad_out = out_grad.astype(jnp.float32)
    part_down = reduce_rows(dense_left(hidden, out_grad))
    grad_hidden = dense_back(out_grad, down_w)
    unused, pull_swiglu = jax.vjp(swiglu, gate_pre, up_pre)
    grad_gate_f, grad_up_f = pull_swiglu(grad_hidden)
    grad_both = jnp.concatenate(
        [grad_gate_f.astype(jnp.bfloat16), grad_up_f.astype(jnp.bfloat16)], axis=1
    )
    grad_both, term_both = lax.optimization_barrier(
        (grad_both, dense_left(normed_ffn, grad_both).astype(jnp.bfloat16))
    )
    part_both = reduce_rows(term_both)
    grad_normed_ffn = dense_back(grad_both, gate_up_w)
    unused, pull_norm_two = jax.vjp(rms_norm, middle, gain_two)
    grad_middle_part, grad_gain_two = pull_norm_two(grad_normed_ffn)
    grad_middle = grad_out + grad_middle_part
    grad_attn = grad_middle.astype(jnp.bfloat16)
    grad_attn, term_output = lax.optimization_barrier(
        (grad_attn, dense_left(gated_rows, grad_attn).astype(jnp.bfloat16))
    )
    part_output = reduce_rows(term_output)
    grad_gated = dense_back(grad_attn, output_w)
    unused, pull_gate = jax.vjp(output_gate, mixed_rows, outgate, head_one)
    mixed_gradient, grad_outgate_f, grad_head = pull_gate(grad_gated)
    grad_outgate = grad_outgate_f.astype(jnp.bfloat16)
    carry_grad = jnp.einsum(
        "thv,thk->hvk",
        heads(mixed_gradient, VALUE_WIDTH),
        heads(query_first, DK),
        precision=high,
    ).reshape(VD, DK)
    outgoing = exchange(carry_grad, decay_all, True)
    grad_qkv, grad_decay = mix_backward(
        seq_start, qkv, cumul, mixed_gradient, saved, outgoing
    )
    grad_logit = (grad_decay * jax.nn.sigmoid(-gate_logit) / normalizer).astype(jnp.bfloat16)
    grad_bias = jnp.sum(grad_logit.astype(jnp.float32), axis=0)
    grad_rank_up = dense_left(rank_rows, grad_logit)
    grad_rank = dense_back(grad_logit, rank_up_w).astype(jnp.bfloat16)
    grad_mixer = jnp.concatenate(
        [grad_qkv, grad_outgate, jnp.pad(grad_rank, ((0, 0), (0, SIDE - rank)))], axis=1
    )
    grad_normed = dense_back(grad_mixer, mixer_w)
    unused, pull_norm_one = jax.vjp(rms_norm, residual_in, gain_one)
    grad_input_part, grad_gain_one = pull_norm_one(grad_normed)
    grad_tokens = (grad_middle + grad_input_part).astype(jnp.bfloat16)

    def spread_rows(vector):
        per = vector.reshape(shards, -1)
        return jnp.pad(per, ((0, 0), (0, rows - per.shape[1]))).reshape(-1, 1)

    small = jnp.concatenate(
        [
            grad_gain_one[:, None],
            grad_gain_two[:, None],
            spread_rows(grad_bias),
            spread_rows(grad_head),
            grad_rank_up.reshape(shards * rows, spread),
        ],
        axis=1,
    )
    term = dense_left(normed, grad_mixer)
    term = term + jnp.pad(small, ((0, 0), (wide + rank, SIDE - rank - small.shape[1])))
    term, part_down, part_both, part_output = lax.optimization_barrier(
        (term.astype(jnp.bfloat16), part_down, part_both, part_output)
    )
    sum_down = gather_rows(part_down)
    sum_both = gather_rows(part_both)
    sum_output = gather_rows(part_output)
    sum_mixer = gather_rows(reduce_rows(term))

    def final(part):
        return part.astype(jnp.float32)

    side_sum = sum_mixer[:, wide:]
    return (
        output,
        grad_tokens,
        final(side_sum[:, at_norm]),
        final(sum_mixer[:, :KD]),
        final(sum_mixer[:, KD : 2 * KD]),
        final(sum_mixer[:, 2 * KD : qkv_width]),
        final(sum_mixer[:, qkv_width:wide]),
        final(side_sum[:, :rank]),
        final(side_sum[:, at_up : at_up + spread].reshape(w_rank_up.shape)),
        final(side_sum[: gate_bias.shape[0], at_bias]),
        final(side_sum[: head_gain.shape[0], at_head]),
        final(sum_output),
        final(side_sum[:, at_ffn]),
        final(sum_both[:, :width]),
        final(sum_both[:, width:]),
        final(sum_down),
    )


def solution(mesh):
    return jax.shard_map(
        per_device,
        mesh=mesh,
        in_specs=(
            P(("replica", "shard"), None),
            P(("replica", "shard")),
            P(("replica", "shard"), None),
            P("shard"),
            P("shard", None),
            P("shard", None),
            P("shard", None),
            P("shard", None),
            P("shard", None),
            P("shard", None),
            P("shard"),
            P("shard"),
            P("shard", None),
            P("shard"),
            P("shard", None),
            P("shard", None),
            P("shard", None),
        ),
        out_specs=(
            P(("replica", "shard"), None),
            P(("replica", "shard"), None),
            P("shard"),
            P("shard", None),
            P("shard", None),
            P("shard", None),
            P("shard", None),
            P("shard", None),
            P("shard", None),
            P("shard"),
            P("shard"),
            P("shard", None),
            P("shard"),
            P("shard", None),
            P("shard", None),
            P("shard", None),
        ),
        check_vma=False,
    )
```

time: 1680 us -> 1100 us (0.65)
  blocking collectives: 406 us -> 78.6 us
  matrix products: 347 us -> 186 us
  local copies, waits for them, and re-layouts: 216 us -> 78.4 us
  waiting for transfers between devices: 472 us -> 582 us
  other arithmetic: 165 us -> 75.4 us
  Pallas kernels: 0 us -> 61 us
  loops' own time: 35.8 us -> 0 us
    reduce_scatter x9 -> x4, waiting for transfers between devices: 121 us -> 429 us  [reduce_rows(): lax.psum_scatter(term.astype(jnp.bfloat16), ROWS, scatter_dimension=0, ti...]
    psum x1 -> x0, blocking collectives: 254 us -> none  [per_device(): lax.psum((summed[0], summed[1], summed[2], summed[3], summed[4], summed[5...]
    all_gather x10 -> x7, waiting for transfers between devices: 346 us -> 147 us  [the longest x4 109 us: fetch(): return lax.all_gather(mine, ROWS, axis=0, tiled=True)]
    dot_general x226 -> x5, matrix products: 162 us -> 8.96 us  [the longest x1 4.26 us: per_device(): jnp.einsum('thv,thk->hvk', heads(mixed_gradient, VALUE_WIDTH), heads(quer...]
    squeeze x96 -> x0, local copies, waits for them, and re-layouts: 63.9 us -> none  [the longest x64 63.7 us: mixer(): lax.scan(jax.checkpoint(block_step), entering_state, shaped)]
    pallas_call x0 -> x4, Pallas kernels: none -> 61 us  [the longest x1 36.8 us: mix_backward(): pl.pallas_call(backward_kernel, grid_spec=pltpu.PrefetchScalarGridSpec(nu...]
    another operation x83 -> x0, other arithmetic: 52.1 us -> none  [the longest x80 49.1 us: block_step(): cumul = jnp.cumsum(log_decay, axis=0)]
    all_gather x6 -> x2, blocking collectives: 124 us -> 78.6 us  [the longest x1 69.9 us: per_device(): decay_all = lax.all_gather(carry_decay, EVERY)]
  transfers between devices with their start and end apart: 19 -> 15, of which waited for: 9 -> 9; matrix products, arithmetic and copies ran while one was open for 32% -> 20% of each run, Pallas kernels for 0% -> 6%
where the time goes in v1:
time: 1100 us; the launch traced here: 1090 us
  waiting for transfers between devices  582 us (53%)
  matrix products  186 us (17%)
  blocking collectives  78.6 us (7%)
  local copies, waits for them, and re-layouts  78.4 us (7%)
  other arithmetic  75.4 us (7%)
  Pallas kernels  61 us (6%)
  between operations  15.6 us (1%)
  starting transfers between devices  12.9 us (1%)
    reduce_scatter x4, waiting for transfers between devices, reduce_rows(): lax.psum_scatter(term.astype(jnp.bfloat16), ROWS, scatter_dimension=0, ti...  429 us
    all_gather x4, waiting for transfers between devices, fetch(): return lax.all_gather(mine, ROWS, axis=0, tiled=True)  109 us
    dot_general x8, matrix products, dense(): return jnp.dot(left, right, preferred_element_type=jnp.float32)  71.1 us
    all_gather x1, blocking collectives, per_device(): decay_all = lax.all_gather(carry_decay, EVERY)  69.9 us
    dot_general x5, matrix products, dense_back(): lax.dot_general(grad_rows, weight, (((1,), (1,)), ((), ())), preferred_el...  56 us
    dot_general x5, matrix products, dense_left(): lax.dot_general(input_rows, grad_rows, (((0,), (0,)), ((), ())), preferre...  49.6 us
    all_gather x3, waiting for transfers between devices, gather_rows(): return lax.all_gather(part, 'replica', axis=0, tiled=True)  38.7 us
    pallas_call x1, Pallas kernels, mix_backward(): pl.pallas_call(backward_kernel, grid_spec=pltpu.PrefetchScalarGridSpec(nu...  36.8 us
  transfers between devices with their start and end apart: 15, of which 9 were waited for; matrix products, arithmetic and copies ran while one was open for 20% of the time, Pallas kernels for 6%

profile of v1, /device:TPU:0, one launch (start us, length us, event | category | flops | bytes accessed | tf_op | source)
XLA Modules:
  0.0 1089.6 jit_solution(9191461460129322192)
XLA Ops:
  12.1 3.8 concatenate.15
  21.7 2.9 copy.184
  26.3 64.4 %all-gather.10.cloned.1.call-done = bf16[1024,3200]{1,0:T(8,128)(2,1)} async-done(((bf16[32,3200]{1,0:T(8,128)(2,1)}), bf16[1024,3200]{1,0:T(8,128)(2,1)}) %all-gather.10.cloned.1.call-update) | async-done | bytes 6553616 | tf_op jit(solution)/shard_map/all_gather | solution.py:284
  95.0 7.3 fusion.28.qkv_ref
  106.0 3.9 copy.224
  123.7 2.9 all-to-all-start
  126.7 2.9 copy.197
  129.6 69.9 %all-gather.1 = f32[32,1,512]{2,1,0:T(1,128)S(1)} all-gather(f32[1,1,512]{2,1,0:T(1,128)S(1)} %bitcast.127), channel_id=2, replica_groups=mesh['replica'=8,'shard'=4] {'replica','shard'}, dimensions={0}, use_global_device_ids=true | all-gather | bytes 67584 | tf_op jit(solution)/shard_map/all_gather | solution.py:387
  205.7 11.9 %fusion.97 = f32[2816,1024]{0,1:T(8,128)} fusion(bf16[2816,1024]{1,0:T(8,128)(2,1)} %all-gather.16.cloned.1.call-done, bf16[1024,1024]{1,0:T(8,128)(2,1)} %param.19), kind=kOutput, calls=%fused_computation.163 | convolution fusion | flops 5905580032 | bytes 19398656 | tf_op jit(solution)/shard_map/dot_general | solution.py:29
  218.6 20.4 %mix_forward.1 = (f32[1024,1024]{1,0:T(8,128)}, f32[16,1024,128]{2,1,0:T(8,128)}) custom-call(s32[1]{0:T(128)} %copy.259.start_ref, bf16[1024,2048]{1,0:T(8,128)(2,1)} %copy-done.4, f32[1024,512]{1,0:T(8,128)} %bitcast.108, bf16[1024,128]{1,0:T(8,128)(2,1)} %bitcast.120), custom_call_target="tpu_custom_call" | custom-call | tf_op jit(solution)/shard_map/mix_forward/pallas_call | solution.py:199
  239.0 5.6 reshape.242
  244.6 3.4 multiply_reduce_fusion.5
  254.1 7.4 multiply_convert_fusion.2
  261.5 5.5 multiply_reduce_fusion.4
  270.7 44.2 %all-gather.14.cloned.1.call-done = bf16[1024,5632]{1,0:T(8,128)(2,1)} async-done(((bf16[32,5632]{1,0:T(8,128)(2,1)}), bf16[1024,5632]{1,0:T(8,128)(2,1)}) %all-gather.14.cloned.1.call-update) | async-done | bytes 11534352 | tf_op jit(solution)/shard_map/all_gather | solution.py:284
  314.9 12.0 %fusion.7 = f32[1024,2816]{1,0:T(8,128)} fusion(bf16[1024,1024]{0,1:T(8,128)(2,1)} %multiply_convert_fusion.1, bf16[1024,5632]{1,0:T(8,128)(2,1)} %all-gather.14.cloned.1.call-done), kind=kOutput, calls=%fused_computation.27 | convolution fusion | flops 5905580032 | bytes 19398656 | tf_op jit(solution)/shard_map/dot_general | solution.py:25
  326.9 22.8 %fusion.3 = (bf16[1024,2816]{1,0:T(8,128)(2,1)}, bf16[1024,2816]{1,0:T(8,128)(2,1)}, bf16[1024,2816]{1,0:T(8,128)(2,1)}) fusion(f32[1024,2816]{1,0:T(8,128)} %fusion.7, f32[2816,1024]{0,1:T(8,128)} %fusion.97, bf16[1024,1024]{0,1:T(8,128)(2,1)} %multiply_convert_fusion.1, bf16[1024,5632]{1,0:T(8,128)(2,1)} %all-gather.14.cloned.1.call-done), kind=kOutput, calls=%fused_computation.6 | convolution fusion | flops 5951717376 | bytes 48234496 | tf_op jit(solution)/shard_map/dot_general | solution.py:25
  349.7 19.7 %convolution_convert_fusion = bf16[1024,5632]{1,0:T(8,128)(2,1)} fusion(bf16[1024,1024]{0,1:T(8,128)(2,1)} %multiply_convert_fusion.1, bf16[1024,2816]{1,0:T(8,128)(2,1)} %get-tuple-element.153, bf16[1024,2816]{1,0:T(8,128)(2,1)} %get-tuple-element.152), kind=kOutput, calls=%fused_computation.14 | convolution fusion | flops 11839995904 | bytes 25165824 | tf_op jit(solution)/shard_map/dot_general | solution.py:35
  369.3 10.1 pad_maximum_fusion
  379.5 18.7 %multiply_reduce_fusion.1 = (f32[1024]{0:T(1024)S(1)}, f32[1024]{0:T(1024)S(1)}, f32[1024,1024]{0,1:T(8,128)S(1)}) fusion(f32[1024,1024]{0,1:T(8,128)S(1)} %copy-done.3, f32[1024]{0:T(1024)S(1)} %fusion.77, f32[1024]{0:T(1024)S(1)} %get-tuple-element.138, bf16[1024,5632]{1,0:T(8,128)(2,1)} %pad_maximum_fusion, ...), kind=kOutput, calls=%fused_computation.49 | convolution fusion | flops 11817449472 | bytes 31473664 | tf_op jit(solution)/shard_map/dot_general | solution.py:29
  401.6 3.7 convolution_convert_fusion.2
  405.4 11.5 %convolution_convert_fusion.1 = bf16[2816,1024]{1,0:T(8,128)(2,1)} fusion(bf16[1024,2816]{1,0:T(8,128)(2,1)} %get-tuple-element.154, bf16[1024,1024]{1,0:T(8,128)(2,1)} %param.19), kind=kOutput, calls=%fused_computation.31 | convolution fusion | flops 5908463616 | bytes 13631488 | tf_op jit(solution)/shard_map/dot_general | solution.py:35
  417.6 11.5 %multiply_reduce_fusion = (f32[1024]{0:T(1024)S(1)}, f32[1024,1024]{1,0:T(8,128)}, bf16[1024,1024]{1,0:T(8,128)(2,1)}) fusion(f32[1024,1024]{1,0:T(8,128)} %get-tuple-element.151, f32[1024,1024]{1,0:T(8,128)} %get-tuple-element.170, f32[1024]{0:T(1024)S(1)} %bitcast.124, bf16[1024,1024]{0,1:T(8,128)(2,1)} %copy-done.16, ...), kind=kOutput, calls=%fused_computation.48 | convolution fusion | flops 2164259840 | bytes 18882560 | tf_op jit(solution)/shard_map/dot_general | solution.py:29
  429.1 5.8 reshape.243
  434.9 4.7 multiply_reduce_fusion.2
  440.1 6.4 add_add_fusion.1
  446.6 4.3 fusion.45
  450.8 3.2 all-to-all-start.2
  455.3 3.0 copy.230
  460.5 3.8 all-to-all-done.2.pieces_ref
  466.9 3.2 all-to-all-start.3
  470.2 10.6 add_add_fusion.2.grad_ref
  481.5 36.8 %mix_backward.1 = (bf16[1024,2048]{1,0:T(8,128)(2,1)}, f32[1024,512]{1,0:T(8,128)}) custom-call(s32[1]{0:T(128)} %copy.259.start_ref, bf16[1024,2048]{1,0:T(8,128)(2,1)} %copy-done.4, f32[1024,512]{1,0:T(8,128)} %bitcast.109, f32[1024,1024]{1,0:T(8,128)} %add_add_fusion.2.grad_ref, f32[16,1024,128]{2,1,0:T(8,128)} %get-tuple-element.31.saved_ref, ...), custom_call_target="tpu_custom_call" | custom-call | tf_op jit(solution)/shard_map/mix_backward/pallas_call | solution.py:226
  518.4 2.9 convert_reduce_fusion
  523.3 13.6 %fusion.14 = (f32[1024]{0:T(1024)S(1)}, f32[1024]{0:T(1024)S(1)}, f32[1024,1024]{0,1:T(8,128)}) fusion(bf16[1024,1024]{0,1:T(8,128)(2,1)} %copy-done.7, f32[1024]{0:T(1024)S(1)} %copy-done.38, f32[1024]{0:T(1024)S(1)} %copy-done.34, bf16[1024,3200]{1,0:T(8,128)(2,1)} %all-gather.10.cloned.1.call-done, bf16[1024,16]{1,0:T(8,128)(2,1)S(1)} %copy.207, ...), kind=kOutput, calls=%fused_computation.35 | convolution fusion | flops 6744438784 | bytes 19185664 | tf_op jit(solution)/shard_map/dot_general | solution.py:29
  541.4 14.5 %add_convert_fusion = bf16[1024,3200]{1,0:T(8,128)(2,1)} fusion(f32[1024,12]{1,0:T(8,128)} %concatenate.19, bf16[1024,16]{1,0:T(8,128)(2,1)S(1)} %copy.207, bf16[1024,1024]{1,0:T(8,128)(2,1)} %get-tuple-element.155, bf16[1024,2048]{1,0:T(8,128)(2,1)} %get-tuple-element.32, bf16[1024,1024]{0,1:T(8,128)(2,1)} %copy-done.7, f32[1024]{0:T(1024)S(1)} %copy-done.34, ...), kind=kOutput, calls=%fused_computation.2 | convolution fusion | flops 6747848704 | bytes 15032320 | tf_op jit(solution)/shard_map/dot_general | solution.py:35
  556.0 130.3 %reduce-scatter.5.cloned.1.call-done = bf16[88,1024]{1,0:T(8,128)(2,1)} async-done(((bf16[2816,1024]{1,0:T(8,128)(2,1)}), bf16[88,1024]{1,0:T(8,128)(2,1)}) %reduce-scatter.5.cloned.1.call-update) | async-done | bytes 180240 | tf_op jit(solution)/shard_map/reduce_scatter | solution.py:288
  686.2 154.7 %reduce-scatter.7.cloned.1.call-done = bf16[32,5632]{1,0:T(8,128)(2,1)} async-done(((bf16[1024,5632]{1,0:T(8,128)(2,1)}), bf16[32,5632]{1,0:T(8,128)(2,1)}) %reduce-scatter.7.cloned.1.call-update) | async-done | bytes 360464 | tf_op jit(solution)/shard_map/reduce_scatter | solution.py:288
  842.3 143.9 %reduce-scatter.11.cloned.1.call-done = bf16[32,3200]{1,0:T(8,128)(2,1)} async-done(((bf16[1024,3200]{1,0:T(8,128)(2,1)}), bf16[32,3200]{1,0:T(8,128)(2,1)}) %reduce-scatter.11.cloned.1.call-update) | async-done | bytes 204816 | tf_op jit(solution)/shard_map/reduce_scatter | solution.py:288
  986.3 11.8 %add_convert_fusion.1 = bf16[1024,1024]{0,1:T(8,128)(2,1)} fusion(f32[1024,1024]{0,1:T(8,128)} %copy-done.2, bf16[1024,2816]{1,0:T(8,128)(2,1)} %get-tuple-element.154, bf16[2816,1024]{1,0:T(8,128)(2,1)} %all-gather.16.cloned.1.call-done), kind=kOutput, calls=%fused_computation.52 | convolution fusion | flops 5907677184 | bytes 17825792 | tf_op jit(solution)/shard_map/dot_general | solution.py:25
  998.0 3.9 copy.215
  1002.0 7.4 fusion.20
  1009.4 4.0 copy.216
  1013.4 8.7 all_gather.34
  1023.2 3.3 convert_element_type.246
  1026.5 15.8 %all-gather.20.cloned.1.call-done = bf16[256,5632]{1,0:T(8,128)(2,1)} async-done(((bf16[32,5632]{1,0:T(8,128)(2,1)}), bf16[256,5632]{1,0:T(8,128)(2,1)}) %all-gather.20.cloned.1.call-update) | async-done | bytes 2883600 | tf_op jit(solution)/shard_map/all_gather | solution.py:292
  1042.2 4.8 slice_convert_fusion
  1047.1 22.9 %all-gather.18.cloned.1.call-done = bf16[256,3200]{1,0:T(8,128)(2,1)} async-done(((bf16[32,3200]{1,0:T(8,128)(2,1)}), bf16[256,3200]{1,0:T(8,128)(2,1)}) %all-gather.18.cloned.1.call-update) | async-done | bytes 1638416 | tf_op jit(solution)/shard_map/all_gather | solution.py:292
  (196 shorter events, 83.2 us)
Async XLA Ops:
  7.2 10.4 copy-start
  7.2 12.8 %copy-start.19 = (bf16[256,2816]{1,0:T(8,128)(2,1)S(1)}, bf16[256,2816]{1,0:T(8,128)(2,1)}, u32[]{:S(2)}) copy-start(bf16[256,2816]{1,0:T(8,128)(2,1)} %param.31) | copy-start | bytes 4325380
  7.2 83.5 %all-gather.10.cloned.1.call-start = ((), (), s32[]{:S(2)}) async-start(), calls=%async_computation.8 | async-start | bytes 6758400 | tf_op jit(solution)/shard_map/all_gather | solution.py:284
  17.6 188.2 %all-gather.16.cloned.1.call-start = ((), (), s32[]{:S(2)}) async-start(), calls=%async_computation.11 | async-start | bytes 5947392 | tf_op jit(solution)/shard_map/all_gather | solution.py:284
  18.4 243.1 %all-gather.12.cloned.1.call-start = ((), (), s32[]{:S(2)}) async-start(), calls=%async_computation.9 | async-start | bytes 2162688 | tf_op jit(solution)/shard_map/all_gather | solution.py:284
  19.9 295.0 %all-gather.14.cloned.1.call-start = ((), (), s32[]{:S(2)}) async-start(), calls=%async_computation.10 | async-start | bytes 11894784 | tf_op jit(solution)/shard_map/all_gather | solution.py:284
  24.6 85.4 %copy-start.7 = (bf16[1024,1024]{0,1:T(8,128)(2,1)}, bf16[1024,1024]{0,1:T(8,128)(2,1)S(1)}, u32[]{:S(2)}) copy-start(bf16[1024,1024]{0,1:T(8,128)(2,1)S(1)} %copy.184) | copy-start | bytes 6291460
  26.3 224.5 %copy-start.37 = (f32[1024]{0:T(1024)}, f32[1024]{0:T(1024)S(1)}, u32[]{:S(2)}) copy-start(f32[1024]{0:T(1024)S(1)} %fusion.76) | copy-start | bytes 12292
  93.6 18.0 %copy-start.26 = (bf16[16,512]{1,0:T(8,128)(2,1)}, bf16[16,512]{1,0:T(8,128)(2,1)S(1)}, u32[]{:S(2)}) copy-start(bf16[16,512]{1,0:T(8,128)(2,1)S(1)} %reshape.235) | copy-start | bytes 49156
  95.0 155.8 %copy-start.33 = (f32[1024]{0:T(1024)}, f32[1024]{0:T(1024)S(1)}, u32[]{:S(2)}) copy-start(f32[1024]{0:T(1024)S(1)} %get-tuple-element.139) | copy-start | bytes 12292
  102.4 2.1 copy-start.4
  110.0 4.3 copy-start.39
  111.6 4.9 copy-start.31
  116.5 5.2 copy-start.6
  116.5 3.1 copy-start.5
  123.7 76.3 %all-to-all-start = ((bf16[32,32,128]{2,1,0:T(8,128)(2,1)}), bf16[32,32,128]{2,1,0:T(8,128)(2,1)S(1)}, u32[]{:S(2)}, u32[]{:S(2)}) async-start(bf16[32,32,128]{2,1,0:T(8,128)(2,1)} %bitcast.8), calls=%async_computation | async-start | bytes 524288 | tf_op jit(solution)/shard_map/all_to_all | solution.py:275
  202.6 15.2 %all-to-all-start.1 = ((bf16[32,32,128]{2,1,0:T(8,128)(2,1)}), bf16[32,32,128]{2,1,0:T(8,128)(2,1)S(1)}, u32[]{:S(2)}, u32[]{:S(2)}) async-start(bf16[32,32,128]{2,1,0:T(8,128)(2,1)} %chain.1), calls=%async_computation.1 | async-start | bytes 524288 | tf_op jit(solution)/shard_map/all_to_all | solution.py:278
  205.2 350.8 %reduce-scatter.9.cloned.1.call-start = ((), (), s32[]{:S(2)}) async-start(), calls=%async_computation.14 | async-start | bytes 2162688 | tf_op jit(solution)/shard_map/reduce_scatter | solution.py:288
  217.8 21.2 %copy-start.35 = (f32[256]{0:T(256)}, f32[256]{0:T(256)S(1)}, u32[]{:S(2)}) copy-start(f32[256]{0:T(256)S(1)} %reshape.254) | copy-start | bytes 3076
  248.2 2.6 copy-start.24
  248.4 2.3 copy-start.14
  249.7 3.3 copy-start.8
  249.7 4.4 copy-start.10
  250.8 2.2 copy-start.11
  369.3 10.1 copy-start.3
  398.2 3.4 copy-start.41
  405.3 280.9 %reduce-scatter.5.cloned.1.call-start = ((), (), s32[]{:S(2)}) async-start(), calls=%async_computation.12 | async-start | bytes 5947392 | tf_op jit(solution)/shard_map/reduce_scatter | solution.py:288
  416.9 424.1 %reduce-scatter.7.cloned.1.call-start = ((), (), s32[]{:S(2)}) async-start(), calls=%async_computation.13 | async-start | bytes 11894784 | tf_op jit(solution)/shard_map/reduce_scatter | solution.py:288
  429.1 5.8 copy-start.36
  434.9 4.9 copy-start.25
  434.9 5.2 copy-start.15
  440.1 6.4 copy-start.12
  450.8 13.5 %all-to-all-start.2 = ((bf16[32,32,128]{2,1,0:T(8,128)(2,1)}), bf16[32,32,128]{2,1,0:T(8,128)(2,1)S(1)}, u32[]{:S(2)}, u32[]{:S(2)}) async-start(bf16[32,32,128]{2,1,0:T(8,128)(2,1)} %bitcast.14), calls=%async_computation.2 | async-start | bytes 524288 | tf_op jit(solution)/shard_map/all_to_all | solution.py:275
  466.9 13.9 %all-to-all-start.3 = ((bf16[32,32,128]{2,1,0:T(8,128)(2,1)}), bf16[32,32,128]{2,1,0:T(8,128)(2,1)S(1)}, u32[]{:S(2)}, u32[]{:S(2)}) async-start(bf16[32,32,128]{2,1,0:T(8,128)(2,1)} %chain_back.1), calls=%async_computation.3 | async-start | bytes 524288 | tf_op jit(solution)/shard_map/all_to_all | solution.py:278
  470.1 516.1 %reduce-scatter.11.cloned.1.call-start = ((), (), s32[]{:S(2)}) async-start(), calls=%async_computation.15 | async-start | bytes 6758400 | tf_op jit(solution)/shard_map/reduce_scatter | solution.py:288
  481.5 36.9 %copy-start.40 = (f32[512]{0:T(512)S(1)}, f32[512]{0:T(512)}, u32[]{:S(2)}) copy-start(f32[512]{0:T(512)} %copy-done.39) | copy-start | bytes 6148
  518.3 3.0 copy-start.32
  518.3 4.4 copy-start.27
  518.3 4.9 copy-start.34
  518.3 4.9 copy-start.38
  523.3 15.6 %copy-start.17 = (f32[1,1024]{0,1:T(8,128)S(1)}, f32[1,1024]{0,1:T(8,128)}, u32[]{:S(2)}) copy-start(f32[1,1024]{0,1:T(8,128)} %copy.234) | copy-start | bytes 12292
  523.3 15.6 %copy-start.18 = (f32[1024,1]{1,0:T(8,128)S(1)}, f32[1024,1]{1,0:T(8,128)}, u32[]{:S(2)}) copy-start(f32[1024,1]{1,0:T(8,128)} %copy.212) | copy-start | bytes 12292
  841.0 182.2 %all-gather.22.cloned.1.call-start = ((), (), s32[]{:S(2)}) async-start(), calls=%async_computation.18 | async-start | bytes 1622016 | tf_op jit(solution)/shard_map/all_gather | solution.py:292
  841.7 200.5 %all-gather.20.cloned.1.call-start = ((), (), s32[]{:S(2)}) async-start(), calls=%async_computation.17 | async-start | bytes 3244032 | tf_op jit(solution)/shard_map/all_gather | solution.py:292
  842.3 227.7 %all-gather.18.cloned.1.call-start = ((), (), s32[]{:S(2)}) async-start(), calls=%async_computation.16 | async-start | bytes 1843200 | tf_op jit(solution)/shard_map/all_gather | solution.py:292
  998.0 3.9 copy-start.30
  1009.4 4.0 copy-start.28
  1042.2 40.4 %copy-start.1 = (bf16[704,1024]{1,0:T(8,128)(2,1)S(1)}, bf16[704,1024]{1,0:T(8,128)(2,1)}, u32[]{:S(2)}) copy-start(bf16[704,1024]{1,0:T(8,128)(2,1)} %param.33) | copy-start | bytes 4325380
  (9 other events, 11.0 us)
Sparse Core Ops, SparseCore 0:
  17.7 72.9 all-gather.9
  94.1 67.6 all-gather.15
  165.2 56.9 all-gather.11
  225.5 89.3 all-gather.13
  405.5 137.2 reduce-scatter.8
  544.9 141.2 reduce-scatter.4
  688.6 152.3 reduce-scatter.6
  843.3 142.9 reduce-scatter.10
  988.1 21.2 all-gather.21
  1011.1 31.0 all-gather.19
  1044.1 25.8 all-gather.17
